TPU v7x, 512 devices: a whole 4x4x16 slice. The times are simulated.
512 devices in a mesh: row: 32 (over x, z_lo), col: 16 (over z_hi, y, core).
Axes of the slice: x: 4, y: 4, z: 16 (z_hi: 2, z_lo: 8; z = z_hi * 8 + z_lo), core: 2. Of those that a mesh axis runs over, the one named last changes fastest.
Arguments:
- amplitudes: float32 [3072, 4, 2048], P(('row', 'col')), may hold values from -6 to 6
- integrals: float32 [8192, 4, 2048], P('row', None, 'col'), may hold values from -0.0625 to 0.0625
Outputs:
- ladder: float32 [3072, 8192], P('col', 'row')
All inputs are finite; a program needn't handle non-finite values.
Results may differ from a plain program's by a relative error of at most 0.0001.
Values sent between devices are 32-bit elements; how exact they have to be, the bound alone decides.
No kernel may reach another device: no remote copies, remote signals or barrier semaphores. Data moves between devices by JAX's collectives and lax.ppermute only.
A program may use at most 64 MiB of HBM per device.

v0:
```python
import jax
import jax.numpy as jnp
from jax import lax
from jax.sharding import PartitionSpec as P

PANELS = 4


def contract(rows, weights):
    return lax.dot_general(
        rows,
        weights,
        (((1,), (1,)), ((), ())),
        precision=lax.Precision.HIGHEST,
        preferred_element_type=jnp.float32,
    )


def per_device(amplitudes, integrals):
    n_row = lax.axis_size("row")
    n_col = lax.axis_size("col")
    local_rows = amplitudes.shape[0]
    width = integrals.shape[2]
    all_rows = local_rows * n_row * n_col
    total = jnp.zeros((all_rows, integrals.shape[0]), jnp.float32)
    for panel in range(PANELS):
        piece = amplitudes[:, panel, :]
        weights = integrals[:, panel, :]
        spread = lax.all_gather(piece, "row", axis=0, tiled=True)
        mixed = lax.all_to_all(spread, "col", split_axis=1, concat_axis=0, tiled=True)
        ordered = (
            mixed.reshape(n_col, n_row, local_rows, width)
            .transpose(1, 0, 2, 3)
            .reshape(all_rows, width)
        )
        total = total + contract(ordered, weights)
    return lax.psum_scatter(total, "col", scatter_dimension=0, tiled=True)


def solution(mesh):
    in_specs = (P(("row", "col"), None, None), P("row", None, "col"))
    out_specs = P("col", "row")
    return jax.shard_map(
        per_device, mesh=mesh, in_specs=in_specs, out_specs=out_specs, check_vma=False
    )
```

profile of v0, /device:TPU:2, one launch (start us, length us, event | category | flops | bytes accessed | tf_op | source)
XLA Modules:
  0.0 1254.1 jit_solution(16290584040939222164)
XLA Ops:
  6.5 2.1 fusion.1
  8.6 212.2 %all-gather.9.cloned.1.call-done = f32[192,1,2048]{2,1,0:T(1,128)} async-done(((f32[6,1,2048]{2,1,0:T(1,128)}), f32[192,1,2048]{2,1,0:T(1,128)}) %all-gather.9.cloned.1.call-update) | async-done | bytes 1572880 | tf_op jit(solution)/shard_map/all_gather | solution.py:29
  220.8 3.1 copy.7
  223.8 14.5 %all-to-all-start = ((f32[192,16,128]{2,0,1:T(8,128)}), f32[192,16,128]{2,0,1:T(8,128)S(1)}, u32[]{:S(2)}, u32[]{:S(2)}) async-start(f32[192,16,128]{2,0,1:T(8,128)} %copy.7), calls=%async_computation | async-start | bytes 3145728 | tf_op jit(solution)/shard_map/all_to_all | solution.py:30
  239.1 246.0 %all-gather.11.cloned.1.call-done = f32[192,1,2048]{2,1,0:T(1,128)} async-done(((f32[6,1,2048]{2,1,0:T(1,128)}), f32[192,1,2048]{2,1,0:T(1,128)}) %all-gather.11.cloned.1.call-update) | async-done | bytes 1572880 | tf_op jit(solution)/shard_map/all_gather | solution.py:29
  485.1 3.1 copy.10
  488.2 7.6 all-to-all-start.1
  496.5 246.0 %all-gather.13.cloned.1.call-done = f32[192,1,2048]{2,1,0:T(1,128)} async-done(((f32[6,1,2048]{2,1,0:T(1,128)}), f32[192,1,2048]{2,1,0:T(1,128)}) %all-gather.13.cloned.1.call-update) | async-done | bytes 1572880 | tf_op jit(solution)/shard_map/all_gather | solution.py:29
  742.6 3.1 copy.13
  746.9 8.1 all-to-all-start.2
  755.6 247.4 %all-gather.15.cloned.1.call-done = f32[192,1,2048]{2,1,0:T(1,128)} async-done(((f32[6,1,2048]{2,1,0:T(1,128)}), f32[192,1,2048]{2,1,0:T(1,128)}) %all-gather.15.cloned.1.call-update) | async-done | bytes 1572880 | tf_op jit(solution)/shard_map/all_gather | solution.py:29
  1002.9 3.1 copy.16
  1006.0 8.0 all-to-all-start.3
  1017.5 2.3 copy.11
  1020.5 1.4 reshape.43
  1021.9 2.3 copy.14
  1024.8 1.4 reshape.45
  1026.2 61.0 %all-to-all-done.3 = f32[192,16,128]{2,0,1:T(8,128)} async-done(((f32[192,16,128]{2,0,1:T(8,128)}), f32[192,16,128]{2,0,1:T(8,128)}, u32[]{:S(2)}, u32[]{:S(2)}) %all-to-all-start.3) | async-done | bytes 1572896 | tf_op jit(solution)/shard_map/all_to_all | solution.py:30
  1087.2 2.3 copy.17
  1091.5 4.2 fusion.2
  1095.7 2.9 convolution_add_fusion.2
  1098.6 2.7 convolution_add_fusion.1
  1101.4 4.3 convolution_add_fusion
  1105.7 141.9 %reduce-scatter.2.cloned.1.call-done = f32[192,256]{1,0:T(8,128)} async-done(((f32[3072,256]{1,0:T(8,128)}), f32[192,256]{1,0:T(8,128)}) %reduce-scatter.2.cloned.1.call-update) | async-done | bytes 196624 | tf_op jit(solution)/shard_map/reduce_scatter | solution.py:37
  (31 shorter events, 9.9 us)
Async XLA Ops:
  6.5 214.2 %all-gather.9.cloned.1.call-start = ((), (), s32[]{:S(2)}) async-start(), calls=%async_computation.6 | async-start | bytes 1622016 | tf_op jit(solution)/shard_map/all_gather | solution.py:29
  223.8 264.3 %all-to-all-start = ((f32[192,16,128]{2,0,1:T(8,128)}), f32[192,16,128]{2,0,1:T(8,128)S(1)}, u32[]{:S(2)}, u32[]{:S(2)}) async-start(f32[192,16,128]{2,0,1:T(8,128)} %copy.7), calls=%async_computation | async-start | bytes 3145728 | tf_op jit(solution)/shard_map/all_to_all | solution.py:30
  238.3 246.8 %all-gather.11.cloned.1.call-start = ((), (), s32[]{:S(2)}) async-start(), calls=%async_computation.7 | async-start | bytes 1622016 | tf_op jit(solution)/shard_map/all_gather | solution.py:29
  488.2 257.5 %all-to-all-start.1 = ((f32[192,16,128]{2,0,1:T(8,128)}), f32[192,16,128]{2,0,1:T(8,128)S(1)}, u32[]{:S(2)}, u32[]{:S(2)}) async-start(f32[192,16,128]{2,0,1:T(8,128)} %copy.10), calls=%async_computation.1 | async-start | bytes 3145728 | tf_op jit(solution)/shard_map/all_to_all | solution.py:30
  495.8 246.8 %all-gather.13.cloned.1.call-start = ((), (), s32[]{:S(2)}) async-start(), calls=%async_computation.8 | async-start | bytes 1622016 | tf_op jit(solution)/shard_map/all_gather | solution.py:29
  745.7 1.2 copy-start
  746.9 259.1 %all-to-all-start.2 = ((f32[192,16,128]{2,0,1:T(8,128)}), f32[192,16,128]{2,0,1:T(8,128)}, u32[]{:S(2)}, u32[]{:S(2)}) async-start(f32[192,16,128]{2,0,1:T(8,128)} %copy.13), calls=%async_computation.2 | async-start | bytes 3145728 | tf_op jit(solution)/shard_map/all_to_all | solution.py:30
  755.0 247.9 %all-gather.15.cloned.1.call-start = ((), (), s32[]{:S(2)}) async-start(), calls=%async_computation.9 | async-start | bytes 1622016 | tf_op jit(solution)/shard_map/all_gather | solution.py:29
  1006.0 8.3 copy-start.4
  1006.0 81.2 %all-to-all-start.3 = ((f32[192,16,128]{2,0,1:T(8,128)}), f32[192,16,128]{2,0,1:T(8,128)}, u32[]{:S(2)}, u32[]{:S(2)}) async-start(f32[192,16,128]{2,0,1:T(8,128)} %copy.16), calls=%async_computation.3 | async-start | bytes 3145728 | tf_op jit(solution)/shard_map/all_to_all | solution.py:30
  1014.0 233.6 %reduce-scatter.2.cloned.1.call-start = ((), (), s32[]{:S(2)}) async-start(), calls=%async_computation.5 | async-start | bytes 3342336 | tf_op jit(solution)/shard_map/reduce_scatter | solution.py:37
  1091.4 4.2 copy-start.1
  1095.7 3.0 copy-start.2
  1098.6 2.7 copy-start.3
Sparse Core Ops, SparseCore 0:
  9.4 211.3 all-gather.8
  241.2 243.8 all-gather.10
  498.7 243.8 all-gather.12
  757.6 245.3 all-gather.14
  1105.8 141.7 reduce-scatter.1
where the time goes:
time: 1250 us
  waiting for transfers between devices  1160 us (93%)
  starting transfers between devices  38.5 us (3%)
  local copies, waits for them, and re-layouts  31.7 us (3%)
  matrix products  14.1 us (1%)
  between operations  13.3 us (1%)
    all_gather x4, waiting for transfers between devices, per_device(): spread = lax.all_gather(piece, 'row', axis=0, tiled=True)  952 us
    reduce_scatter x1, waiting for transfers between devices, per_device(): return lax.psum_scatter(total, 'col', scatter_dimension=0, tiled=True)  142 us
    all_to_all x4, waiting for transfers between devices, per_device(): lax.all_to_all(spread, 'col', split_axis=1, concat_axis=0, tiled=True)  61 us
    all_to_all x4, starting transfers between devices, per_device(): lax.all_to_all(spread, 'col', split_axis=1, concat_axis=0, tiled=True)  38.2 us
  transfers between devices with their start and end apart: 9, of which 6 were waited for; matrix products, arithmetic and copies ran while one was open for 2% of the time, Pallas kernels for 0%

commit v1 on v0

--- a/solution.py
+++ b/solution.py
@@ -26,7 +26,9 @@
     for panel in range(PANELS):
         piece = amplitudes[:, panel, :]
         weights = integrals[:, panel, :]
-        spread = lax.all_gather(piece, "row", axis=0, tiled=True)
+        spread = jnp.concatenate(
+            lax.all_to_all(jnp.stack([piece] * lax.axis_size("row")), "row", 0, 0), axis=0
+        )
         mixed = lax.all_to_all(spread, "col", split_axis=1, concat_axis=0, tiled=True)
         ordered = (
             mixed.reshape(n_col, n_row, local_rows, width)

time: 1250 us -> 926 us (0.74)
  waiting for transfers between devices: 1160 us -> 771 us
  starting transfers between devices: 38.5 us -> 83.8 us
    all_gather x4 -> x0, waiting for transfers between devices: 952 us -> none  [per_device(): spread = lax.all_gather(piece, 'row', axis=0, tiled=True)]
    all_to_all x0 -> x4, waiting for transfers between devices: none -> 357 us  [per_device(): lax.all_to_all(jnp.stack([piece] * lax.axis_size('row')), 'row', 0, 0)]
    all_to_all x4, waiting for transfers between devices: 61 us -> 192 us  [per_device(): lax.all_to_all(spread, 'col', split_axis=1, concat_axis=0, tiled=True)]
    reduce_scatter x1, waiting for transfers between devices: 142 us -> 222 us  [per_device(): return lax.psum_scatter(total, 'col', scatter_dimension=0, tiled=True)]
    all_to_all x0 -> x4, starting transfers between devices: none -> 50.2 us  [per_device(): lax.all_to_all(jnp.stack([piece] * lax.axis_size('row')), 'row', 0, 0)]
    all_to_all x8 -> x12, local copies, waits for them, and re-layouts: 20.2 us -> 25.6 us  [per_device(): lax.all_to_all(spread, 'col', split_axis=1, concat_axis=0, tiled=True)]
  transfers between devices with their start and end apart: 9 -> 9, of which waited for: 6 -> 9; matrix products, arithmetic and copies ran while one was open for 2% -> 2% of each run, Pallas kernels for 0% -> 0%
where the time goes in v1:
time: 926 us; the launch traced here: 925 us
  waiting for transfers between devices  771 us (83%)
  starting transfers between devices  83.8 us (9%)
  local copies, waits for them, and re-layouts  42.9 us (5%)
  matrix products  14.2 us (2%)
  between operations  13.6 us (1%)
    all_to_all x4, waiting for transfers between devices, per_device(): lax.all_to_all(jnp.stack([piece] * lax.axis_size('row')), 'row', 0, 0)  357 us
    reduce_scatter x1, waiting for transfers between devices, per_device(): return lax.psum_scatter(total, 'col', scatter_dimension=0, tiled=True)  222 us
    all_to_all x4, waiting for transfers between devices, per_device(): lax.all_to_all(spread, 'col', split_axis=1, concat_axis=0, tiled=True)  192 us
    all_to_all x4, starting transfers between devices, per_device(): lax.all_to_all(jnp.stack([piece] * lax.axis_size('row')), 'row', 0, 0)  50.2 us
    all_to_all x4, starting transfers between devices, per_device(): lax.all_to_all(spread, 'col', split_axis=1, concat_axis=0, tiled=True)  33.4 us
    all_to_all x12, local copies, waits for them, and re-layouts, per_device(): lax.all_to_all(spread, 'col', split_axis=1, concat_axis=0, tiled=True)  25.6 us
  transfers between devices with their start and end apart: 9, of which 9 were waited for; matrix products, arithmetic and copies ran while one was open for 2% of the time, Pallas kernels for 0%

profile of v1, /device:TPU:2, one launch (start us, length us, event | category | flops | bytes accessed | tf_op | source)
XLA Modules:
  0.0 925.2 jit_solution(8790647642855032254)
XLA Ops:
  9.6 15.7 %all-to-all-start = ((f32[32,6,2048]{2,1,0:T(8,128)}), f32[32,6,2048]{2,1,0:T(8,128)S(1)}, u32[]{:S(2)}, u32[]{:S(2)}) async-start(f32[32,6,2048]{2,1,0:T(8,128)} %stack.12), calls=%async_computation | async-start | bytes 4194304 | tf_op jit(solution)/shard_map/all_to_all | solution.py:30
  25.3 90.8 %all-to-all-done = f32[32,6,2048]{2,1,0:T(8,128)S(1)} async-done(((f32[32,6,2048]{2,1,0:T(8,128)}), f32[32,6,2048]{2,1,0:T(8,128)S(1)}, u32[]{:S(2)}, u32[]{:S(2)}) %all-to-all-start) | async-done | bytes 1572896 | tf_op jit(solution)/shard_map/all_to_all | solution.py:30
  117.6 11.5 %all-to-all-start.2 = ((f32[32,6,2048]{2,1,0:T(8,128)}), f32[32,6,2048]{2,1,0:T(8,128)}, u32[]{:S(2)}, u32[]{:S(2)}) async-start(f32[32,6,2048]{2,1,0:T(8,128)} %stack.13), calls=%async_computation.2 | async-start | bytes 4194304 | tf_op jit(solution)/shard_map/all_to_all | solution.py:30
  129.2 90.6 %all-to-all-done.2 = f32[32,6,2048]{2,1,0:T(8,128)} async-done(((f32[32,6,2048]{2,1,0:T(8,128)}), f32[32,6,2048]{2,1,0:T(8,128)}, u32[]{:S(2)}, u32[]{:S(2)}) %all-to-all-start.2) | async-done | bytes 1572896 | tf_op jit(solution)/shard_map/all_to_all | solution.py:30
  221.4 11.5 %all-to-all-start.4 = ((f32[32,6,2048]{2,1,0:T(8,128)}), f32[32,6,2048]{2,1,0:T(8,128)}, u32[]{:S(2)}, u32[]{:S(2)}) async-start(f32[32,6,2048]{2,1,0:T(8,128)} %stack.14), calls=%async_computation.4 | async-start | bytes 4194304 | tf_op jit(solution)/shard_map/all_to_all | solution.py:30
  232.9 90.1 %all-to-all-done.4 = f32[32,6,2048]{2,1,0:T(8,128)} async-done(((f32[32,6,2048]{2,1,0:T(8,128)}), f32[32,6,2048]{2,1,0:T(8,128)}, u32[]{:S(2)}, u32[]{:S(2)}) %all-to-all-start.4) | async-done | bytes 1572896 | tf_op jit(solution)/shard_map/all_to_all | solution.py:30
  324.6 11.6 %all-to-all-start.6 = ((f32[32,6,2048]{2,1,0:T(8,128)}), f32[32,6,2048]{2,1,0:T(8,128)}, u32[]{:S(2)}, u32[]{:S(2)}) async-start(f32[32,6,2048]{2,1,0:T(8,128)} %stack.15), calls=%async_computation.6 | async-start | bytes 4194304 | tf_op jit(solution)/shard_map/all_to_all | solution.py:30
  337.9 3.1 copy.24
  341.0 85.4 %all-to-all-done.6 = f32[32,6,2048]{2,1,0:T(8,128)} async-done(((f32[32,6,2048]{2,1,0:T(8,128)}), f32[32,6,2048]{2,1,0:T(8,128)}, u32[]{:S(2)}, u32[]{:S(2)}) %all-to-all-start.6) | async-done | bytes 1572896 | tf_op jit(solution)/shard_map/all_to_all | solution.py:30
  426.4 10.3 %all-to-all-start.1 = ((f32[192,16,128]{2,0,1:T(8,128)}), f32[192,16,128]{2,0,1:T(8,128)S(1)}, u32[]{:S(2)}, u32[]{:S(2)}) async-start(f32[192,16,128]{2,0,1:T(8,128)} %copy.24), calls=%async_computation.1 | async-start | bytes 3145728 | tf_op jit(solution)/shard_map/all_to_all | solution.py:32
  440.3 31.3 %all-to-all-done.1 = f32[192,16,128]{2,0,1:T(8,128)S(1)} async-done(((f32[192,16,128]{2,0,1:T(8,128)}), f32[192,16,128]{2,0,1:T(8,128)S(1)}, u32[]{:S(2)}, u32[]{:S(2)}) %all-to-all-start.1) | async-done | bytes 1572896 | tf_op jit(solution)/shard_map/all_to_all | solution.py:32
  471.6 3.7 all-to-all-start.3
  475.3 2.8 all_to_all.69
  478.1 3.1 copy.32
  481.2 52.6 %all-to-all-done.3 = f32[192,16,128]{2,0,1:T(8,128)S(1)} async-done(((f32[192,16,128]{2,0,1:T(8,128)}), f32[192,16,128]{2,0,1:T(8,128)S(1)}, u32[]{:S(2)}, u32[]{:S(2)}) %all-to-all-start.3) | async-done | bytes 1572896 | tf_op jit(solution)/shard_map/all_to_all | solution.py:32
  535.0 14.0 %all-to-all-start.5 = ((f32[192,16,128]{2,0,1:T(8,128)}), f32[192,16,128]{2,0,1:T(8,128)}, u32[]{:S(2)}, u32[]{:S(2)}) async-start(f32[192,16,128]{2,0,1:T(8,128)} %copy.32), calls=%async_computation.5 | async-start | bytes 3145728 | tf_op jit(solution)/shard_map/all_to_all | solution.py:32
  552.5 58.3 %all-to-all-done.5 = f32[192,16,128]{2,0,1:T(8,128)} async-done(((f32[192,16,128]{2,0,1:T(8,128)}), f32[192,16,128]{2,0,1:T(8,128)}, u32[]{:S(2)}, u32[]{:S(2)}) %all-to-all-start.5) | async-done | bytes 1572896 | tf_op jit(solution)/shard_map/all_to_all | solution.py:32
  610.9 5.3 all-to-all-start.7
  628.3 50.0 %all-to-all-done.7 = f32[192,16,128]{2,0,1:T(8,128)} async-done(((f32[192,16,128]{2,0,1:T(8,128)}), f32[192,16,128]{2,0,1:T(8,128)}, u32[]{:S(2)}, u32[]{:S(2)}) %all-to-all-start.7) | async-done | bytes 1572896 | tf_op jit(solution)/shard_map/all_to_all | solution.py:32
  682.6 4.2 fusion.2
  686.8 2.9 convolution_add_fusion.2
  689.8 2.7 convolution_add_fusion.1
  692.5 4.3 convolution_add_fusion
  696.9 221.5 %reduce-scatter.2.cloned.1.call-done = f32[192,256]{1,0:T(8,128)} async-done(((f32[3072,256]{1,0:T(8,128)}), f32[192,256]{1,0:T(8,128)}) %reduce-scatter.2.cloned.1.call-update) | async-done | bytes 196624 | tf_op jit(solution)/shard_map/reduce_scatter | solution.py:39
  (39 shorter events, 34.1 us)
Async XLA Ops:
  9.6 106.5 %all-to-all-start = ((f32[32,6,2048]{2,1,0:T(8,128)}), f32[32,6,2048]{2,1,0:T(8,128)S(1)}, u32[]{:S(2)}, u32[]{:S(2)}) async-start(f32[32,6,2048]{2,1,0:T(8,128)} %stack.12), calls=%async_computation | async-start | bytes 4194304 | tf_op jit(solution)/shard_map/all_to_all | solution.py:30
  117.6 102.2 %all-to-all-start.2 = ((f32[32,6,2048]{2,1,0:T(8,128)}), f32[32,6,2048]{2,1,0:T(8,128)}, u32[]{:S(2)}, u32[]{:S(2)}) async-start(f32[32,6,2048]{2,1,0:T(8,128)} %stack.13), calls=%async_computation.2 | async-start | bytes 4194304 | tf_op jit(solution)/shard_map/all_to_all | solution.py:30
  221.4 101.7 %all-to-all-start.4 = ((f32[32,6,2048]{2,1,0:T(8,128)}), f32[32,6,2048]{2,1,0:T(8,128)}, u32[]{:S(2)}, u32[]{:S(2)}) async-start(f32[32,6,2048]{2,1,0:T(8,128)} %stack.14), calls=%async_computation.4 | async-start | bytes 4194304 | tf_op jit(solution)/shard_map/all_to_all | solution.py:30
  324.6 101.8 %all-to-all-start.6 = ((f32[32,6,2048]{2,1,0:T(8,128)}), f32[32,6,2048]{2,1,0:T(8,128)}, u32[]{:S(2)}, u32[]{:S(2)}) async-start(f32[32,6,2048]{2,1,0:T(8,128)} %stack.15), calls=%async_computation.6 | async-start | bytes 4194304 | tf_op jit(solution)/shard_map/all_to_all | solution.py:30
  426.4 45.2 %all-to-all-start.1 = ((f32[192,16,128]{2,0,1:T(8,128)}), f32[192,16,128]{2,0,1:T(8,128)S(1)}, u32[]{:S(2)}, u32[]{:S(2)}) async-start(f32[192,16,128]{2,0,1:T(8,128)} %copy.24), calls=%async_computation.1 | async-start | bytes 3145728 | tf_op jit(solution)/shard_map/all_to_all | solution.py:32
  471.6 62.2 %all-to-all-start.3 = ((f32[192,16,128]{2,0,1:T(8,128)}), f32[192,16,128]{2,0,1:T(8,128)S(1)}, u32[]{:S(2)}, u32[]{:S(2)}) async-start(f32[192,16,128]{2,0,1:T(8,128)} %copy.28), calls=%async_computation.3 | async-start | bytes 3145728 | tf_op jit(solution)/shard_map/all_to_all | solution.py:32
  533.8 1.2 copy-start
  535.0 75.9 %all-to-all-start.5 = ((f32[192,16,128]{2,0,1:T(8,128)}), f32[192,16,128]{2,0,1:T(8,128)}, u32[]{:S(2)}, u32[]{:S(2)}) async-start(f32[192,16,128]{2,0,1:T(8,128)} %copy.32), calls=%async_computation.5 | async-start | bytes 3145728 | tf_op jit(solution)/shard_map/all_to_all | solution.py:32
  552.5 63.9 %copy-start.4 = (f32[256,4,128]{2,1,0:T(4,128)S(1)}, f32[256,4,128]{2,1,0:T(4,128)}, u32[]{:S(2)}) copy-start(f32[256,4,128]{2,1,0:T(4,128)} %param.3) | copy-start | bytes 1572868
  610.9 67.5 %all-to-all-start.7 = ((f32[192,16,128]{2,0,1:T(8,128)}), f32[192,16,128]{2,0,1:T(8,128)}, u32[]{:S(2)}, u32[]{:S(2)}) async-start(f32[192,16,128]{2,0,1:T(8,128)} %copy.36), calls=%async_computation.7 | async-start | bytes 3145728 | tf_op jit(solution)/shard_map/all_to_all | solution.py:32
  616.2 302.2 %reduce-scatter.2.cloned.1.call-start = ((), (), s32[]{:S(2)}) async-start(), calls=%async_computation.9 | async-start | bytes 3342336 | tf_op jit(solution)/shard_map/reduce_scatter | solution.py:39
  682.6 4.2 copy-start.1
  686.8 3.0 copy-start.2
  689.8 2.7 copy-start.3
Sparse Core Ops, SparseCore 0:
  697.0 221.3 reduce-scatter.1
